TPU v7x, 128 devices: a whole 4x4x4 slice. The times are simulated.
128 devices in a mesh: outer: 8 (over z, core), inner: 16 (over y, x).
Axes of the slice: x: 4, y: 4, z: 4, core: 2. Of those that a mesh axis runs over, the one named last changes fastest.
Arguments:
- tokens_in: bfloat16 [16384, 2048], P(('outer', 'inner')), may hold values from -6 to 6
- expert_ids: int32 [16384, 10], P(('outer', 'inner')), may hold values from 0 to 255, all different within a row; in each aligned block of 128 rows (0 to 127, 128 to 255, ...) at most 6 rows name the same one
- route_weight: float32 [16384, 10], P(('outer', 'inner')), may hold values from 0.05 to 1
- first_gain: float32 [2048], replicated, may hold values from 0.5 to 1.5
- gate_weight: bfloat16 [256, 2048, 512], P(('outer', 'inner')), may hold values from -0.125 to 0.125
- up_weight: bfloat16 [256, 2048, 512], P(('outer', 'inner')), may hold values from -0.125 to 0.125
- down_weight: bfloat16 [256, 512, 2048], P(('outer', 'inner')), may hold values from -0.25 to 0.25
- second_gain: float32 [2048], replicated, may hold values from 0.5 to 1.5
- mixer_weight: bfloat16 [2048, 4096], P(None, 'inner'), may hold values from -0.125 to 0.125
- gating_weight: bfloat16 [2048, 32], replicated, may hold values from -0.125 to 0.125
- filter_taps: bfloat16 [4, 4096], replicated, may hold values from -3 to 3
- decay_log: float32 [16], replicated, may hold values from -9 to -3
- decay_bias: float32 [16], replicated, may hold values from -1 to 1
- output_gain: float32 [128], replicated, may hold values from 0.5 to 1.5
Outputs:
- hidden_out: bfloat16 [16384, 2048], P(('outer', 'inner'))
- core_out: bfloat16 [16384, 2048], P(('outer', 'inner'))
Inputs may be any that keep to these rules, and one draw needn't show every extreme that they name: `expert_ids`: each token names 10 different experts; the 128 rows of one device name any one expert at most 6 times, a bound that some block reaches.
All inputs are finite; a program needn't handle non-finite values.
Results may differ from a plain program's by a relative error of at most 0.015.
Values may be sent and summed in bfloat16 or wider, within the bound.
A program may use at most 576 MiB of HBM per device.

v0:
```python
import jax
import jax.numpy as jnp
from jax import lax
from jax.sharding import PartitionSpec as P


def shifted(value, axis, steps):
    count = lax.axis_size(axis)
    leading, last = (max(0, -steps), min(count, count - steps))
    return lax.ppermute(value, axis, [(source, source + steps) for source in range(leading, last)])


def prefix_2(x, axis, join, neutral):
    place = lax.axis_index(axis)
    gathered = jax.tree.map(
        lambda a, kind: lax.all_gather(a.astype(kind), axis), x, (jnp.bfloat16, jnp.bfloat16)
    )
    state = jax.tree.map(lambda a, e: jnp.zeros_like(a) + jnp.asarray(e, a.dtype), x, neutral)

    def one(lap, state):
        return join(
            state,
            jax.tree.map(
                lambda a, own: lax.dynamic_index_in_dim(a, lap, 0, False).astype(own.dtype),
                gathered,
                x,
            ),
        )

    return lax.fori_loop(0, place, one, state)


def shortened(x):

    def short(part):
        return part.astype(jnp.bfloat16) if part.dtype == jnp.float32 else part

    return jax.tree.map(short, x)


def spread_2(value, axis, source):
    kept = jnp.where(lax.axis_index(axis) == source, value, 0).astype(value.dtype)
    return lax.psum(kept, axis)


def entering(x, axis, combine, identity):
    length, place = (lax.axis_size(axis), lax.axis_index(axis))
    everything = jax.tree.map(
        lambda part, kind: lax.all_gather(part.astype(kind), axis),
        x,
        jax.tree.map(lambda a: jnp.bfloat16 if a.dtype == jnp.float32 else a.dtype, x),
    )
    start = jax.tree.map(
        lambda part, zero: jnp.broadcast_to(jnp.asarray(zero, part.dtype), part.shape), x, identity
    )

    def lap(k, before):
        reached = k < place
        new = combine(
            before, jax.tree.map(lambda part, own: part[k].astype(own.dtype), everything, x)
        )
        return jax.tree.map(lambda a, b: jnp.where(reached, a, b), new, before)

    return lax.fori_loop(0, length, lap, start)


def rms_scale(values, gain):
    wide = values.astype(jnp.float32)
    return wide * lax.rsqrt(jnp.mean(wide * wide, axis=-1, keepdims=True) + 1e-06) * gain


def unit_heads(values):
    return values * lax.rsqrt(jnp.sum(values * values, axis=-1, keepdims=True) + 1e-06)


def run_experts(piece, gate_weight, up_weight, down_weight):
    gate = jnp.einsum("secd,edf->secf", piece, gate_weight, preferred_element_type=jnp.float32)
    upper = jnp.einsum("secd,edf->secf", piece, up_weight, preferred_element_type=jnp.float32)
    hidden = (jax.nn.silu(gate) * upper).astype(jnp.bfloat16)
    return jnp.einsum(
        "secf,efd->secd", hidden, down_weight, preferred_element_type=jnp.float32
    ).astype(jnp.bfloat16)


def join_maps(earlier, later):
    first_map, first_state = earlier
    next_map, next_state = later
    joined_map = jnp.einsum("hij,hjk->hik", next_map, first_map, precision=lax.Precision.HIGHEST)
    joined_state = (
        jnp.einsum("hij,hjv->hiv", next_map, first_state, precision=lax.Precision.HIGHEST)
        + next_state
    )
    return (joined_map, joined_state)


def per_device(
    tokens_in,
    expert_ids,
    route_weight,
    first_gain,
    gate_weight,
    up_weight,
    down_weight,
    second_gain,
    mixer_weight,
    gating_weight,
    filter_taps,
    decay_log,
    decay_bias,
    output_gain,
):
    n_outer = lax.axis_size("outer")
    n_inner = lax.axis_size("inner")
    n_dev = n_outer * n_inner
    tok_count, width = tokens_in.shape
    top_count = expert_ids.shape[1]
    local_experts = gate_weight.shape[0]
    experts_all = local_experts * n_dev
    capacity = max(2, 6 * tok_count * top_count // (5 * experts_all))
    normed_first = rms_scale(tokens_in, first_gain).astype(jnp.bfloat16)
    mix_weight = route_weight / jnp.sum(route_weight, axis=1, keepdims=True)
    pairs = tok_count * top_count
    flat = expert_ids.reshape(-1)
    onehot = (flat[:, None] == jnp.arange(experts_all, dtype=jnp.int32)[None, :]).astype(jnp.int32)
    before = jnp.cumsum(onehot, axis=0) - onehot
    slot_index = jnp.sum(before * onehot, axis=1)
    target = (
        flat // local_experts * (local_experts * capacity)
        + flat % local_experts * capacity
        + slot_index
    )
    owner = jnp.arange(pairs, dtype=jnp.int32) // top_count
    outgoing = (
        jnp.zeros((n_dev * local_experts * capacity, width), jnp.bfloat16)
        .at[target]
        .set(normed_first[owner])
    )
    outgoing = outgoing.reshape(n_dev, local_experts, capacity, width)
    served = run_experts(
        lax.all_to_all(outgoing, ("outer", "inner"), split_axis=0, concat_axis=0, tiled=True),
        gate_weight,
        up_weight,
        down_weight,
    )
    returned = lax.all_to_all(served, ("outer", "inner"), split_axis=0, concat_axis=0, tiled=True)
    rows_back = (
        returned.reshape(-1, width)[target].astype(jnp.float32) * mix_weight.reshape(-1)[:, None]
    )
    mixture = jnp.sum(rows_back.reshape(tok_count, top_count, width), axis=1)
    hidden_out = (tokens_in.astype(jnp.float32) + mixture).astype(jnp.bfloat16)
    normed_second = rms_scale(hidden_out, second_gain).astype(jnp.bfloat16)
    mixed = jnp.dot(
        normed_second,
        lax.all_gather(mixer_weight, "inner", axis=1, tiled=True),
        preferred_element_type=jnp.float32,
    )
    projected = mixed.astype(jnp.bfloat16)
    gating = jnp.dot(normed_second, gating_weight, preferred_element_type=jnp.float32)
    taps = filter_taps.shape[0]
    rim = shifted(projected[tok_count - (taps - 1) :], ("outer", "inner"), 1)
    padded = jnp.concatenate([rim, projected], axis=0).astype(jnp.float32)
    filtered = jnp.zeros(projected.shape, jnp.float32)
    for tap_index in range(taps):
        filtered = (
            filtered
            + filter_taps[tap_index].astype(jnp.float32) * padded[tap_index : tap_index + tok_count]
        )
    filtered = jax.nn.silu(filtered)
    head_dim = output_gain.shape[0]
    value_heads = decay_log.shape[0]
    key_heads = (projected.shape[1] - value_heads * head_dim) // (2 * head_dim)
    ratio = value_heads // key_heads
    queries = unit_heads(
        filtered[:, : key_heads * head_dim].reshape(tok_count, key_heads, head_dim)
    ) * head_dim ** (-0.5)
    keys = unit_heads(
        filtered[:, key_heads * head_dim : 2 * key_heads * head_dim].reshape(
            tok_count, key_heads, head_dim
        )
    )
    values = filtered[:, 2 * key_heads * head_dim :].reshape(tok_count, value_heads, head_dim)
    queries = jnp.repeat(queries, ratio, axis=1)
    keys = jnp.repeat(keys, ratio, axis=1)
    strength = jax.nn.sigmoid(gating[:, :value_heads]).T
    log_decay = (-jnp.exp(decay_log) * jax.nn.softplus(gating[:, value_heads:] + decay_bias)).T
    cumulative = jnp.cumsum(log_decay, axis=1)
    positions = jnp.arange(tok_count)
    lower_incl = positions[:, None] >= positions[None, :]
    lower_strict = positions[:, None] > positions[None, :]
    spread = cumulative[:, :, None] - cumulative[:, None, :]
    decay_mat = jnp.where(lower_incl, jnp.exp(jnp.where(lower_incl, spread, 0.0)), 0.0)
    key_major = keys.transpose(1, 0, 2)
    query_leading = queries.transpose(1, 0, 2)
    value_major = values.transpose(1, 0, 2)
    key_inner = jnp.einsum("htd,hid->hti", key_major, key_major, precision=lax.Precision.HIGHEST)
    lower_part = jnp.where(lower_strict, decay_mat * key_inner, 0.0) * strength[:, :, None]
    system = lower_part + jnp.eye(tok_count, dtype=jnp.float32)
    growth = jnp.exp(cumulative)
    scaled_keys = key_major * (strength * growth)[:, :, None]
    scaled_values = value_major * strength[:, :, None]
    key_resolved = lax.linalg.triangular_solve(
        system, scaled_keys, left_side=True, lower=True, unit_diagonal=True
    )
    value_resolved = lax.linalg.triangular_solve(
        system, scaled_values, left_side=True, lower=True, unit_diagonal=True
    )
    tail = jnp.exp(cumulative[:, -1:] - cumulative)
    trailing_keys = key_major * tail[:, :, None]
    eye_heads = jnp.broadcast_to(
        jnp.eye(head_dim, dtype=jnp.float32), (value_heads, head_dim, head_dim)
    )
    state_map = growth[:, -1][:, None, None] * eye_heads - jnp.einsum(
        "htk,htj->hkj", trailing_keys, key_resolved, precision=lax.Precision.HIGHEST
    )
    state_increment = jnp.einsum(
        "xbe,xbz->xez", trailing_keys, value_resolved, precision=lax.Precision.HIGHEST
    )
    identity = (eye_heads, jnp.zeros_like(state_increment))
    inner_pre = prefix_2((state_map, state_increment), "inner", join_maps, identity)
    inclusive = join_maps(inner_pre, (state_map, state_increment))
    group = spread_2(shortened(jnp.stack(inclusive)), "inner", n_inner - 1)
    outer_pre = entering((group[0], group[1]), "outer", join_maps, identity)
    prefix = join_maps(outer_pre, inner_pre)
    initial_state = prefix[1]
    updates = value_resolved - jnp.einsum(
        "mwx,mxd->mwd", key_resolved, initial_state, precision=lax.Precision.HIGHEST
    )
    query_key = (
        jnp.einsum("htd,hid->hti", query_leading, key_major, precision=lax.Precision.HIGHEST)
        * decay_mat
    )
    carried = (
        jnp.einsum("mwx,mxd->mwd", query_leading, initial_state, precision=lax.Precision.HIGHEST)
        * growth[:, :, None]
    )
    attended = carried + jnp.einsum(
        "hti,hiv->htv", query_key, updates, precision=lax.Precision.HIGHEST
    )
    attended = attended.transpose(1, 0, 2)
    core_out = (
        rms_scale(attended, output_gain)
        .astype(jnp.bfloat16)
        .reshape(tok_count, value_heads * head_dim)
    )
    return (hidden_out, core_out)


def solution(mesh):
    return jax.shard_map(
        per_device,
        mesh=mesh,
        in_specs=(
            P(("outer", "inner"), None),
            P(("outer", "inner"), None),
            P(("outer", "inner"), None),
            P(),
            P(("outer", "inner"), None, None),
            P(("outer", "inner"), None, None),
            P(("outer", "inner"), None, None),
            P(),
            P(None, "inner"),
            P(),
            P(),
            P(),
            P(),
            P(),
        ),
        out_specs=(P(("outer", "inner"), None), P(("outer", "inner"), None)),
        check_vma=False,
    )
```

profile of v0, /device:TPU:1, one launch (start us, length us, event | category | flops | bytes accessed | tf_op | source)
XLA Modules:
  0.0 936.2 jit_solution(5289336182392275664)
XLA Ops:
  7.2 0.7 all-gather.8.cloned.1.call-update
  7.9 0.8 copy.70
  9.2 0.3 fusion.32
  9.9 0.8 copy.74
  10.7 0.5 fusion.52
  11.7 34.4 %scatter_custom_fusion = bf16[1536,2048]{1,0:T(8,128)(2,1)} fusion(s32[1280]{0:T(1024)S(1)} %fusion.80, bf16[128,2048]{1,0:T(8,128)(2,1)S(1)} %fusion.61, s32[2048]{0:T(1024)S(1)} %pad_clamp_fusion.1, bf16[]{:T(256)} %constant.104.clone.1), kind=kCustom, calls=%fused_computation.26 | custom fusion | bytes 6291458 | tf_op jit(solution)/shard_map/scatter | solution.py:136
  46.1 11.0 %reshape.311 = bf16[128,2,6,2048]{3,2,1,0:T(8,128)(2,1)} reshape(bf16[1536,2048]{1,0:T(8,128)(2,1)} %scatter_custom_fusion) | data formatting | bytes 12582912 | tf_op jit(solution)/shard_map/reshape | solution.py:138
  57.1 9.6 %copy.75 = bf16[128,2,6,2048]{3,1,2,0:T(2,128)(2,1)S(1)} copy(bf16[128,2,6,2048]{3,2,1,0:T(8,128)(2,1)} %reshape.311) | data formatting | bytes 12582912 | tf_op jit(solution)/shard_map/reshape | solution.py:138
  66.7 110.7 %all_to_all.10 = bf16[128,2,6,2048]{3,1,2,0:T(2,128)(2,1)S(1)} all-to-all(bf16[128,2,6,2048]{3,1,2,0:T(2,128)(2,1)S(1)} %copy.75), channel_id=1, replica_groups=mesh['outer'=8,'inner'=16] {'outer','inner'}, dimensions={0} | all-to-all | bytes 12582912 | tf_op jit(solution)/shard_map/all_to_all | solution.py:140
  177.5 2.6 copy-done.8
  180.1 8.6 fusion.15
  188.7 19.6 %convert_bitcast_fusion = bf16[128,2,6,2048]{3,0,2,1:T(8,128)(2,1)} fusion(bf16[2,512,2048]{2,1,0:T(8,128)(2,1)} %param.26, f32[2,128,6,512]{3,1,2,0:T(8,128)} %fusion.15, bf16[2,2048,512]{2,1,0:T(8,128)(2,1)} %param.24, bf16[128,2,6,2048]{3,1,2,0:T(2,128)(2,1)} %copy-done.8), kind=kOutput, calls=%fused_computation.21 | convolution fusion | flops 6450315264 | bytes 24117248 | tf_op jit(solution)/shard_map/secf,efd->secd/dot_general | solution.py:80
  208.4 12.8 %copy.78 = bf16[128,2,6,2048]{3,1,2,0:T(2,128)(2,1)} copy(bf16[128,2,6,2048]{3,0,2,1:T(8,128)(2,1)} %convert_bitcast_fusion) | data formatting | bytes 12582912 | tf_op jit(solution)/shard_map/convert_element_type | solution.py:82
  221.1 7.9 all-to-all-start.1
  229.5 74.2 %all-to-all-done.1 = bf16[128,2,6,2048]{3,1,2,0:T(2,128)(2,1)} async-done(((bf16[128,2,6,2048]{3,1,2,0:T(2,128)(2,1)}), bf16[128,2,6,2048]{3,1,2,0:T(2,128)(2,1)}, u32[]{:S(2)}, u32[]{:S(2)}) %all-to-all-start.1) | async-done | bytes 6291488 | tf_op jit(solution)/shard_map/all_to_all | solution.py:145
  303.7 10.4 %copy.79 = bf16[128,2,6,2048]{3,2,1,0:T(8,128)(2,1)} copy(bf16[128,2,6,2048]{3,1,2,0:T(2,128)(2,1)} %all-to-all-done.1) | data formatting | bytes 12582912 | tf_op jit(solution)/shard_map/all_to_all | solution.py:145
  314.1 11.4 %reshape.312 = bf16[1536,2048]{1,0:T(8,128)(2,1)} reshape(bf16[128,2,6,2048]{3,2,1,0:T(8,128)(2,1)} %copy.79) | data formatting | bytes 12582912 | tf_op jit(solution)/shard_map/reshape | solution.py:147
  325.5 14.4 %gather_fusion = bf16[1280,2048]{1,0:T(8,128)(2,1)} fusion(bf16[1536,2048]{1,0:T(8,128)(2,1)} %reshape.312, s32[2048]{0:T(1024)S(1)} %pad_clamp_fusion), kind=kCustom, calls=%fused_computation.1 | custom fusion | bytes 10490880 | tf_op jit(solution)/shard_map/gather | solution.py:147
  339.9 10.3 %reshape.322 = f32[128,10,2048]{2,1,0:T(8,128)} reshape(bf16[1280,2048]{1,0:T(8,128)(2,1)} %gather_fusion) | data formatting | bytes 15728640 | tf_op jit(solution)/shard_map/convert_element_type | solution.py:147
  350.3 9.5 %multiply_reduce_fusion = f32[128,2048]{1,0:T(8,128)S(1)} fusion(f32[128,10,2048]{2,1,0:T(8,128)} %reshape.322, f32[128,10]{1,0:T(8,128)S(1)} %copy.80), kind=kLoop, calls=%fused_computation.20 | loop fusion | flops 4980736 | bytes 11539456 | tf_op jit(solution)/shard_map/reduce_sum | solution.py:149
  360.1 0.3 fusion.69
  361.0 8.2 convolution_convert_fusion
  369.3 4.0 collective-permute-start
  373.4 4.5 collective-permute-done
  378.3 1.2 divide_multiply_fusion
  379.5 1.0 slice_bitcast_fusion
  381.3 1.0 copy-done.12
  382.2 3.4 fusion.50
  385.6 157.9 %custom-call.5 = f32[16,1,128,128]{2,3,1,0:T(8,128)S(1)} custom-call(f32[16,1,128,128]{3,2,1,0:T(8,128)} %fusion.50), custom_call_target="InvertDiagBlocksLowerTriangular" | custom-call | tf_op jit(solution)/shard_map/triangular_solve/custom-call.1 | solution.py:201
  543.6 1.3 copy.86
  544.9 1.6 copy.87
  546.5 2.1 fusion.63
  548.6 1.6 bitcast_multiply_fusion.4
  550.3 3.0 fusion.89
  553.8 3.1 fusion.65
  556.9 2.8 fusion.88
  559.7 60.0 %all-gather.16.cloned.1.call-done = bf16[256,128,128]{2,1,0:T(8,128)(2,1)} async-done(((bf16[16,128,128]{2,1,0:T(8,128)(2,1)}), bf16[256,128,128]{2,1,0:T(8,128)(2,1)}) %all-gather.16.cloned.1.call-update) | async-done | bytes 8388624 | tf_op jit(solution)/shard_map/all_gather | solution.py:16
  619.7 72.5 %all-gather.14.cloned.1.call-done = bf16[256,128,128]{2,1,0:T(8,128)(2,1)} async-done(((bf16[16,128,128]{2,1,0:T(8,128)(2,1)}), bf16[256,128,128]{2,1,0:T(8,128)(2,1)}) %all-gather.14.cloned.1.call-update) | async-done | bytes 8388624 | tf_op jit(solution)/shard_map/all_gather | solution.py:16
  692.4 1.1 fusion.54
  693.6 2.4 fusion.55
  696.0 1.1 maximum_select_fusion
  697.2 141.7 %all-reduce.2.cloned.1.call-done = bf16[2,16,128,128]{3,2,1,0:T(8,128)(2,1)} async-done(((bf16[2,16,128,128]{3,2,1,0:T(8,128)(2,1)}), bf16[2,16,128,128]{3,2,1,0:T(8,128)(2,1)}) %all-reduce.2.cloned.1.call-update) | async-done | bytes 1048592 | tf_op jit(solution)/shard_map/psum | solution.py:43
  838.9 2.3 fusion.87
  841.2 0.3 all-gather.12.cloned.1.call-start
  842.6 1.0 copy-done.1
  843.6 3.3 convolution_multiply_fusion
  846.9 27.9 %all-gather.10.cloned.1.call-done = bf16[8,16,128,128]{3,2,1,0:T(8,128)(2,1)} async-done(((bf16[1,16,128,128]{3,2,1,0:T(8,128)(2,1)}), bf16[8,16,128,128]{3,2,1,0:T(8,128)(2,1)}) %all-gather.10.cloned.1.call-update) | async-done | bytes 4194320 | tf_op jit(solution)/shard_map/all_gather | solution.py:49
  874.8 33.7 %all-gather.12.cloned.1.call-done = bf16[8,16,128,128]{3,2,1,0:T(8,128)(2,1)} async-done(((bf16[1,16,128,128]{3,2,1,0:T(8,128)(2,1)}), bf16[8,16,128,128]{3,2,1,0:T(8,128)(2,1)}) %all-gather.12.cloned.1.call-update) | async-done | bytes 4194320 | tf_op jit(solution)/shard_map/all_gather | solution.py:49
  908.6 12.7 %while.27 = (s32[]{:T(128)}, bf16[16,128,128]{2,1,0:T(8,128)(2,1)S(1)}, s32[]{:T(128)}, bf16[8,16,128,128]{3,2,1,0:T(8,128)(2,1)}, bf16[8,16,128,128]{3,2,1,0:T(8,128)(2,1)}, /*index=5*/s32[]{:T(128)}, s32[]{:T(128)}) while((s32[]{:T(128)}, bf16[16,128,128]{2,1,0:T(8,128)(2,1)S(1)}, s32[]{:T(128)}, ...), condition=%wide.region_15.17_spmd.clone, body=%wide.region_14.16_spmd.clone.sunk | while | flops 68157440 | bytes 3672671 | solution.py:64
  908.6 1.5 fusion.130
  910.2 1.5 fusion.130
  911.8 1.5 fusion.130
  913.4 1.5 fusion.130
  915.0 1.5 fusion.130
  916.5 1.5 fusion.130
  918.1 1.5 fusion.130
  919.7 1.5 fusion.130
  921.3 0.7 convolution_add_fusion.2
  921.9 0.5 copy-done.4
  922.5 0.3 copy-done.6
  922.8 1.2 convolution_subtract_fusion
  924.0 1.9 fusion.44
  925.9 1.9 multiply_reduce_fusion.1
  928.0 1.0 copy.92
  (116 shorter events, 6.0 us)
Async XLA Ops:
  7.2 352.9 %copy-start = (bf16[2048,32]{0,1:T(8,128)(2,1)S(1)}, bf16[2048,32]{0,1:T(8,128)(2,1)}, u32[]{:S(2)}) copy-start(bf16[2048,32]{0,1:T(8,128)(2,1)} %param.29) | copy-start | bytes 393220
  7.2 353.8 %all-gather.8.cloned.1.call-start = ((), (), s32[]{:S(2)}) async-start(), calls=%async_computation.2 | async-start | bytes 17825792 | tf_op jit(solution)/shard_map/all_gather | solution.py:154
  9.6 1.6 copy-start.9
  9.6 1.8 copy-start.20
  66.7 113.4 %copy-start.23 = (bf16[2,2048,512]{2,1,0:T(8,128)(2,1)S(1)}, bf16[2,2048,512]{2,1,0:T(8,128)(2,1)}, u32[]{:S(2)}) copy-start(bf16[2,2048,512]{2,1,0:T(8,128)(2,1)} %param.25) | copy-start | bytes 12582916
  177.5 2.6 copy-start.8
  221.1 8.0 copy-start.19
  221.1 8.2 copy-start.24
  221.1 8.4 copy-start.17
  221.1 82.6 %all-to-all-start.1 = ((bf16[128,2,6,2048]{3,1,2,0:T(2,128)(2,1)}), bf16[128,2,6,2048]{3,1,2,0:T(2,128)(2,1)}, u32[]{:S(2)}, u32[]{:S(2)}) async-start(bf16[128,2,6,2048]{3,1,2,0:T(2,128)(2,1)} %copy.78), calls=%async_computation.1 | async-start | bytes 12582912 | tf_op jit(solution)/shard_map/all_to_all | solution.py:145
  229.1 390.6 %all-gather.16.cloned.1.call-start = ((), (), s32[]{:S(2)}) async-start(), calls=%async_computation.7 | async-start | bytes 8912896 | tf_op jit(solution)/shard_map/all_gather | solution.py:16
  350.3 9.8 %copy-start.18 = (f32[2048]{0:T(1024)S(1)}, f32[2048]{0:T(1024)}, u32[]{:S(2)}) copy-start(f32[2048]{0:T(1024)} %param.27) | copy-start | bytes 24580
  350.3 10.2 %copy-start.21 = (f32[16]{0:T(128)S(1)}, f32[16]{0:T(128)}, u32[]{:S(2)}) copy-start(f32[16]{0:T(128)} %param.32) | copy-start | bytes 196
  360.0 9.2 copy-start.15
  369.3 8.6 collective-permute-start
  379.5 1.7 copy-start.7
  381.2 1.0 copy-start.12
  381.2 162.4 %slice-start = ((f32[128,4096]{1,0:T(8,128)}), f32[128,2048]{1,0:T(8,128)S(1)}, s32[]{:S(2)}) async-start(f32[128,4096]{1,0:T(8,128)} %copy-done.7), calls=%async_computation.8 | async-start | bytes 2097152 | tf_op jit(solution)/shard_map/slice | solution.py:181
  543.6 6.7 copy-start.10
  548.6 1.7 copy-start.3
  550.3 3.5 copy-start.11
  553.4 138.8 %all-gather.14.cloned.1.call-start = ((), (), s32[]{:S(2)}) async-start(), calls=%async_computation.6 | async-start | bytes 8912896 | tf_op jit(solution)/shard_map/all_gather | solution.py:16
  556.9 135.3 %copy-start.5 = (f32[16,128,128]{2,1,0:T(8,128)}, f32[16,128,128]{2,1,0:T(8,128)S(1)}, u32[]{:S(2)}) copy-start(f32[16,128,128]{2,1,0:T(8,128)S(1)} %fusion.65) | copy-start | bytes 3145732
  559.6 279.2 %all-reduce.2.cloned.1.call-start = ((), (), s32[]{:S(2)}) async-start(), calls=%async_computation.3 | async-start | bytes 2097152 | tf_op jit(solution)/shard_map/psum | solution.py:43
  696.0 145.8 %copy-start.16 = (f32[16,8,8,128]{3,1,2,0:T(8,128)S(1)}, f32[16,8,8,128]{3,1,2,0:T(8,128)}, u32[]{:S(2)}) copy-start(f32[16,8,8,128]{3,1,2,0:T(8,128)} %get-tuple-element.185) | copy-start | bytes 1572868
  697.1 177.7 %all-gather.10.cloned.1.call-start = ((), (), s32[]{:S(2)}) async-start(), calls=%async_computation.4 | async-start | bytes 4718592 | tf_op jit(solution)/shard_map/all_gather | solution.py:49
  841.2 67.4 %all-gather.12.cloned.1.call-start = ((), (), s32[]{:S(2)}) async-start(), calls=%async_computation.5 | async-start | bytes 4718592 | tf_op jit(solution)/shard_map/all_gather | solution.py:49
  841.8 1.8 copy-start.13
  842.6 1.1 copy-start.1
  921.2 1.2 copy-start.4
  921.2 1.5 copy-start.6
  921.2 2.7 copy-start.2
  922.8 3.1 copy-start.14
  924.0 3.9 copy-start.22
Sparse Core Ops, SparseCore 0:
  10.1 187.0 all-gather.7
  553.5 66.1 all-gather.15
  621.8 70.3 all-gather.13
  697.2 141.5 all-reduce.1
  841.3 33.4 all-gather.9
  876.4 32.1 all-gather.11
where the time goes:
time: 942 us; the launch traced here: 936 us
  waiting for transfers between devices  416 us (44%)
  other arithmetic  175 us (19%)
  local copies, waits for them, and re-layouts  131 us (14%)
  blocking collectives  111 us (12%)
  matrix products  75.8 us (8%)
  between operations  15.1 us (2%)
  starting transfers between devices  12.7 us (1%)
    another operation x4, other arithmetic, per_device(): lax.linalg.triangular_solve(system, scaled_keys, left_side=True, lower=Tr...  158 us
    psum x1, waiting for transfers between devices, spread_2(): return lax.psum(kept, axis)  142 us
    all_gather x2, waiting for transfers between devices, prefix_2(): lax.all_gather(a.astype(kind), axis)  132 us
    all_to_all x1, blocking collectives, per_device(): lax.all_to_all(outgoing, ('outer', 'inner'), split_axis=0, concat_axis=0,...  111 us
    all_to_all x1, waiting for transfers between devices, per_device(): lax.all_to_all(served, ('outer', 'inner'), split_axis=0, concat_axis=0, t...  74.2 us
    all_gather x2, waiting for transfers between devices, entering(): lax.all_gather(part.astype(kind), axis)  61.6 us
    scatter x1, local copies, waits for them, and re-layouts, per_device(): outgoing = jnp.zeros((n_dev * local_experts * capacity, width), jnp.bfloa...  34.4 us
    reshape x2, local copies, waits for them, and re-layouts, per_device(): outgoing = outgoing.reshape(n_dev, local_experts, capacity, width)  20.6 us
  transfers between devices with their start and end apart: 8, of which 7 were waited for; matrix products, arithmetic and copies ran while one was open for 18% of the time, Pallas kernels for 0%

commit v1 on v0

--- a/solution.py
+++ b/solution.py
@@ -40,7 +40,7 @@
 
 def spread_2(value, axis, source):
     kept = jnp.where(lax.axis_index(axis) == source, value, 0).astype(value.dtype)
-    return lax.psum(kept, axis)
+    return jnp.sum(lax.all_gather(kept, axis), axis=0)
 
 
 def entering(x, axis, combine, identity):

time: 942 us -> 975 us (1.035)
  waiting for transfers between devices: 416 us -> 439 us
  other arithmetic: 175 us -> 185 us
    all_gather x0 -> x1, waiting for transfers between devices: none -> 167 us  [spread_2(): return jnp.sum(lax.all_gather(kept, axis), axis=0)]
    psum x1 -> x0, waiting for transfers between devices: 142 us -> none  [spread_2(): return lax.psum(kept, axis)]
  transfers between devices with their start and end apart: 8 -> 8, of which waited for: 7 -> 7; matrix products, arithmetic and copies ran while one was open for 18% -> 17% of each run, Pallas kernels for 0% -> 0%
where the time goes in v1:
time: 975 us; the launch traced here: 969 us
  waiting for transfers between devices  439 us (45%)
  other arithmetic  185 us (19%)
  local copies, waits for them, and re-layouts  131 us (13%)
  blocking collectives  111 us (11%)
  matrix products  75.8 us (8%)
  between operations  15.1 us (2%)
  starting transfers between devices  12.7 us (1%)
    all_gather x1, waiting for transfers between devices, spread_2(): return jnp.sum(lax.all_gather(kept, axis), axis=0)  167 us
    another operation x4, other arithmetic, per_device(): lax.linalg.triangular_solve(system, scaled_keys, left_side=True, lower=Tr...  158 us
    all_gather x2, waiting for transfers between devices, prefix_2(): lax.all_gather(a.astype(kind), axis)  132 us
    all_to_all x1, blocking collectives, per_device(): lax.all_to_all(outgoing, ('outer', 'inner'), split_axis=0, concat_axis=0,...  111 us
    all_to_all x1, waiting for transfers between devices, per_device(): lax.all_to_all(served, ('outer', 'inner'), split_axis=0, concat_axis=0, t...  74.2 us
    all_gather x2, waiting for transfers between devices, entering(): lax.all_gather(part.astype(kind), axis)  59.5 us
    scatter x1, local copies, waits for them, and re-layouts, per_device(): outgoing = jnp.zeros((n_dev * local_experts * capacity, width), jnp.bfloa...  34.4 us
    reshape x2, local copies, waits for them, and re-layouts, per_device(): outgoing = outgoing.reshape(n_dev, local_experts, capacity, width)  20.6 us
  transfers between devices with their start and end apart: 8, of which 7 were waited for; matrix products, arithmetic and copies ran while one was open for 17% of the time, Pallas kernels for 0%

profile of v1, /device:TPU:1, one launch (start us, length us, event | category | flops | bytes accessed | tf_op | source)
XLA Modules:
  0.0 969.0 jit_solution(7619046856805840864)
XLA Ops:
  7.2 0.7 all-gather.9.cloned.1.call-update
  7.9 0.8 copy.70
  9.2 0.3 fusion.32
  9.9 0.8 copy.74
  10.7 0.5 fusion.52
  11.7 34.4 %scatter_custom_fusion = bf16[1536,2048]{1,0:T(8,128)(2,1)} fusion(s32[1280]{0:T(1024)S(1)} %fusion.80, bf16[128,2048]{1,0:T(8,128)(2,1)S(1)} %fusion.61, s32[2048]{0:T(1024)S(1)} %pad_clamp_fusion.1, bf16[]{:T(256)} %constant.105.clone.1), kind=kCustom, calls=%fused_computation.26 | custom fusion | bytes 6291458 | tf_op jit(solution)/shard_map/scatter | solution.py:136
  46.1 11.0 %reshape.347 = bf16[128,2,6,2048]{3,2,1,0:T(8,128)(2,1)} reshape(bf16[1536,2048]{1,0:T(8,128)(2,1)} %scatter_custom_fusion) | data formatting | bytes 12582912 | tf_op jit(solution)/shard_map/reshape | solution.py:138
  57.1 9.6 copy.75
  66.7 110.7 %all_to_all.10 = bf16[128,2,6,2048]{3,1,2,0:T(2,128)(2,1)S(1)} all-to-all(bf16[128,2,6,2048]{3,1,2,0:T(2,128)(2,1)S(1)} %copy.75), channel_id=1, replica_groups=mesh['outer'=8,'inner'=16] {'outer','inner'}, dimensions={0} | all-to-all | bytes 12582912 | tf_op jit(solution)/shard_map/all_to_all | solution.py:140
  177.5 2.6 copy-done.9
  180.1 8.6 fusion.15
  188.7 19.6 %convert_bitcast_fusion = bf16[128,2,6,2048]{3,0,2,1:T(8,128)(2,1)} fusion(bf16[2,512,2048]{2,1,0:T(8,128)(2,1)} %param.26, f32[2,128,6,512]{3,1,2,0:T(8,128)} %fusion.15, bf16[2,2048,512]{2,1,0:T(8,128)(2,1)} %param.24, bf16[128,2,6,2048]{3,1,2,0:T(2,128)(2,1)} %copy-done.9), kind=kOutput, calls=%fused_computation.21 | convolution fusion | flops 6450315264 | bytes 24117248 | tf_op jit(solution)/shard_map/secf,efd->secd/dot_general | solution.py:80
  208.4 12.8 %copy.78 = bf16[128,2,6,2048]{3,1,2,0:T(2,128)(2,1)} copy(bf16[128,2,6,2048]{3,0,2,1:T(8,128)(2,1)} %convert_bitcast_fusion) | data formatting | bytes 12582912 | tf_op jit(solution)/shard_map/convert_element_type | solution.py:82
  221.1 7.9 all-to-all-start.1
  229.5 74.2 %all-to-all-done.1 = bf16[128,2,6,2048]{3,1,2,0:T(2,128)(2,1)} async-done(((bf16[128,2,6,2048]{3,1,2,0:T(2,128)(2,1)}), bf16[128,2,6,2048]{3,1,2,0:T(2,128)(2,1)}, u32[]{:S(2)}, u32[]{:S(2)}) %all-to-all-start.1) | async-done | bytes 6291488 | tf_op jit(solution)/shard_map/all_to_all | solution.py:145
  303.7 10.4 %copy.79 = bf16[128,2,6,2048]{3,2,1,0:T(8,128)(2,1)} copy(bf16[128,2,6,2048]{3,1,2,0:T(2,128)(2,1)} %all-to-all-done.1) | data formatting | bytes 12582912 | tf_op jit(solution)/shard_map/all_to_all | solution.py:145
  314.1 11.4 %reshape.348 = bf16[1536,2048]{1,0:T(8,128)(2,1)} reshape(bf16[128,2,6,2048]{3,2,1,0:T(8,128)(2,1)} %copy.79) | data formatting | bytes 12582912 | tf_op jit(solution)/shard_map/reshape | solution.py:147
  325.5 14.4 %gather_fusion = bf16[1280,2048]{1,0:T(8,128)(2,1)} fusion(bf16[1536,2048]{1,0:T(8,128)(2,1)} %reshape.348, s32[2048]{0:T(1024)S(1)} %pad_clamp_fusion), kind=kCustom, calls=%fused_computation.1 | custom fusion | bytes 10490880 | tf_op jit(solution)/shard_map/gather | solution.py:147
  339.9 10.3 %reshape.358 = f32[128,10,2048]{2,1,0:T(8,128)} reshape(bf16[1280,2048]{1,0:T(8,128)(2,1)} %gather_fusion) | data formatting | bytes 15728640 | tf_op jit(solution)/shard_map/convert_element_type | solution.py:147
  350.3 9.5 multiply_reduce_fusion
  360.1 0.3 fusion.69
  361.0 8.2 convolution_convert_fusion
  369.3 4.0 collective-permute-start
  373.4 4.5 collective-permute-done
  378.2 1.2 divide_multiply_fusion
  379.5 1.0 slice_bitcast_fusion
  381.2 1.0 copy-done.13
  382.2 3.4 fusion.50
  385.6 157.9 %custom-call.5 = f32[16,1,128,128]{2,3,1,0:T(8,128)S(1)} custom-call(f32[16,1,128,128]{3,2,1,0:T(8,128)} %fusion.50), custom_call_target="InvertDiagBlocksLowerTriangular" | custom-call | tf_op jit(solution)/shard_map/triangular_solve/custom-call.1 | solution.py:201
  543.6 1.3 copy.86
  544.9 1.6 copy.87
  546.5 2.1 fusion.63
  548.6 1.6 bitcast_multiply_fusion.4
  550.3 3.0 fusion.89
  553.8 3.1 fusion.65
  556.9 2.8 fusion.88
  559.7 60.0 %all-gather.19.cloned.1.call-done = bf16[256,128,128]{2,1,0:T(8,128)(2,1)} async-done(((bf16[16,128,128]{2,1,0:T(8,128)(2,1)}), bf16[256,128,128]{2,1,0:T(8,128)(2,1)}) %all-gather.19.cloned.1.call-update) | async-done | bytes 8388624 | tf_op jit(solution)/shard_map/all_gather | solution.py:16
  619.7 72.5 %all-gather.17.cloned.1.call-done = bf16[256,128,128]{2,1,0:T(8,128)(2,1)} async-done(((bf16[16,128,128]{2,1,0:T(8,128)(2,1)}), bf16[256,128,128]{2,1,0:T(8,128)(2,1)}) %all-gather.17.cloned.1.call-update) | async-done | bytes 8388624 | tf_op jit(solution)/shard_map/all_gather | solution.py:16
  692.4 1.1 fusion.54
  693.6 2.4 fusion.55
  696.0 1.1 maximum_select_fusion
  697.2 167.4 %all-gather.11.cloned.1.call-done = bf16[16,2,16,128,128]{4,3,2,1,0:T(8,128)(2,1)} async-done(((bf16[1,2,16,128,128]{4,3,2,1,0:T(8,128)(2,1)}), bf16[16,2,16,128,128]{4,3,2,1,0:T(8,128)(2,1)}) %all-gather.11.cloned.1.call-update) | async-done | bytes 16777232 | tf_op jit(solution)/shard_map/all_gather | solution.py:43
  864.6 9.3 reduce_sum.94
  873.9 1.1 fusion.87
  875.6 1.2 copy.102
  877.5 1.0 copy-done.2
  878.5 3.3 convolution_multiply_fusion
  881.8 25.8 %all-gather.13.cloned.1.call-done = bf16[8,16,128,128]{3,2,1,0:T(8,128)(2,1)} async-done(((bf16[1,16,128,128]{3,2,1,0:T(8,128)(2,1)}), bf16[8,16,128,128]{3,2,1,0:T(8,128)(2,1)}) %all-gather.13.cloned.1.call-update) | async-done | bytes 4194320 | tf_op jit(solution)/shard_map/all_gather | solution.py:49
  907.6 33.7 %all-gather.15.cloned.1.call-done = bf16[8,16,128,128]{3,2,1,0:T(8,128)(2,1)} async-done(((bf16[1,16,128,128]{3,2,1,0:T(8,128)(2,1)}), bf16[8,16,128,128]{3,2,1,0:T(8,128)(2,1)}) %all-gather.15.cloned.1.call-update) | async-done | bytes 4194320 | tf_op jit(solution)/shard_map/all_gather | solution.py:49
  941.4 12.7 %while.27 = (s32[]{:T(128)}, bf16[16,128,128]{2,1,0:T(8,128)(2,1)S(1)}, s32[]{:T(128)}, bf16[8,16,128,128]{3,2,1,0:T(8,128)(2,1)}, bf16[8,16,128,128]{3,2,1,0:T(8,128)(2,1)}, /*index=5*/s32[]{:T(128)}, s32[]{:T(128)}) while((s32[]{:T(128)}, bf16[16,128,128]{2,1,0:T(8,128)(2,1)S(1)}, s32[]{:T(128)}, ...), condition=%wide.region_15.17_spmd.clone, body=%wide.region_14.16_spmd.clone.sunk | while | flops 68157440 | bytes 3672671 | solution.py:64
  941.4 1.5 fusion.130
  943.0 1.5 fusion.130
  944.6 1.5 fusion.130
  946.2 1.5 fusion.130
  947.8 1.5 fusion.130
  949.3 1.5 fusion.130
  950.9 1.5 fusion.130
  952.5 1.5 fusion.130
  954.1 0.7 convolution_add_fusion.2
  954.7 0.5 copy-done.5
  955.6 1.2 convolution_subtract_fusion
  956.8 1.9 fusion.44
  958.7 1.9 multiply_reduce_fusion.1
  960.9 1.0 copy.92
  (117 shorter events, 6.5 us)
Async XLA Ops:
  7.2 352.9 %copy-start = (bf16[2048,32]{0,1:T(8,128)(2,1)S(1)}, bf16[2048,32]{0,1:T(8,128)(2,1)}, u32[]{:S(2)}) copy-start(bf16[2048,32]{0,1:T(8,128)(2,1)} %param.29) | copy-start | bytes 393220
  7.2 353.8 %all-gather.9.cloned.1.call-start = ((), (), s32[]{:S(2)}) async-start(), calls=%async_computation.2 | async-start | bytes 17825792 | tf_op jit(solution)/shard_map/all_gather | solution.py:154
  9.6 1.6 copy-start.10
  9.6 1.8 copy-start.20
  66.7 113.4 %copy-start.23 = (bf16[2,2048,512]{2,1,0:T(8,128)(2,1)S(1)}, bf16[2,2048,512]{2,1,0:T(8,128)(2,1)}, u32[]{:S(2)}) copy-start(bf16[2,2048,512]{2,1,0:T(8,128)(2,1)} %param.25) | copy-start | bytes 12582916
  177.5 2.6 copy-start.9
  221.1 8.0 copy-start.19
  221.1 8.2 copy-start.24
  221.1 8.4 copy-start.17
  221.1 82.6 %all-to-all-start.1 = ((bf16[128,2,6,2048]{3,1,2,0:T(2,128)(2,1)}), bf16[128,2,6,2048]{3,1,2,0:T(2,128)(2,1)}, u32[]{:S(2)}, u32[]{:S(2)}) async-start(bf16[128,2,6,2048]{3,1,2,0:T(2,128)(2,1)} %copy.78), calls=%async_computation.1 | async-start | bytes 12582912 | tf_op jit(solution)/shard_map/all_to_all | solution.py:145
  229.1 390.6 %all-gather.19.cloned.1.call-start = ((), (), s32[]{:S(2)}) async-start(), calls=%async_computation.7 | async-start | bytes 8912896 | tf_op jit(solution)/shard_map/all_gather | solution.py:16
  350.2 9.8 %copy-start.18 = (f32[2048]{0:T(1024)S(1)}, f32[2048]{0:T(1024)}, u32[]{:S(2)}) copy-start(f32[2048]{0:T(1024)} %param.27) | copy-start | bytes 24580
  350.3 10.2 %copy-start.21 = (f32[16]{0:T(128)S(1)}, f32[16]{0:T(128)}, u32[]{:S(2)}) copy-start(f32[16]{0:T(128)} %param.32) | copy-start | bytes 196
  360.0 9.2 copy-start.16
  369.3 8.6 collective-permute-start
  379.5 1.7 copy-start.8
  381.2 1.0 copy-start.13
  381.2 162.4 %slice-start = ((f32[128,4096]{1,0:T(8,128)}), f32[128,2048]{1,0:T(8,128)S(1)}, s32[]{:S(2)}) async-start(f32[128,4096]{1,0:T(8,128)} %copy-done.8), calls=%async_computation.8 | async-start | bytes 2097152 | tf_op jit(solution)/shard_map/slice | solution.py:181
  543.6 6.7 copy-start.11
  548.6 1.7 copy-start.4
  550.3 3.5 copy-start.12
  553.3 138.8 %all-gather.17.cloned.1.call-start = ((), (), s32[]{:S(2)}) async-start(), calls=%async_computation.6 | async-start | bytes 8912896 | tf_op jit(solution)/shard_map/all_gather | solution.py:16
  556.9 135.3 %copy-start.6 = (f32[16,128,128]{2,1,0:T(8,128)}, f32[16,128,128]{2,1,0:T(8,128)S(1)}, u32[]{:S(2)}) copy-start(f32[16,128,128]{2,1,0:T(8,128)S(1)} %fusion.65) | copy-start | bytes 3145732
  559.6 305.0 %all-gather.11.cloned.1.call-start = ((), (), s32[]{:S(2)}) async-start(), calls=%async_computation.3 | async-start | bytes 17825792 | tf_op jit(solution)/shard_map/all_gather | solution.py:43
  697.1 210.5 %all-gather.13.cloned.1.call-start = ((), (), s32[]{:S(2)}) async-start(), calls=%async_computation.4 | async-start | bytes 4718592 | tf_op jit(solution)/shard_map/all_gather | solution.py:49
  875.0 66.4 %all-gather.15.cloned.1.call-start = ((), (), s32[]{:S(2)}) async-start(), calls=%async_computation.5 | async-start | bytes 4718592 | tf_op jit(solution)/shard_map/all_gather | solution.py:49
  875.6 3.0 copy-start.14
  877.5 1.1 copy-start.2
  954.0 1.2 copy-start.5
  954.0 1.5 copy-start.7
  954.1 2.7 copy-start.3
  955.6 3.1 copy-start.15
  956.8 3.9 copy-start.22
  956.8 5.1 copy-start.1
Sparse Core Ops, SparseCore 0:
  10.1 187.0 all-gather.8
  553.5 66.1 all-gather.18
  621.8 70.3 all-gather.16
  697.2 167.3 all-gather.10
  875.1 32.4 all-gather.12
  909.2 32.1 all-gather.14
